TPU v7x, 32 devices: a whole 2x2x4 slice. The times are simulated.
32 devices in a mesh: pp: 2 (over core), fsdp: 4 (over y, x), tp: 4 (over z).
Axes of the slice: x: 2, y: 2, z: 4, core: 2. Of those that a mesh axis runs over, the one named last changes fastest.
Arguments:
- inputs: bfloat16 [2, 128, 8192], P(None, 'tp', 'fsdp'), may hold values from -12 to 12
- head_grad: bfloat16 [2, 128, 8192], P(None, 'tp', 'fsdp'), may hold values from -0.3 to 0.3
- noise_mask: int32 [2, 128], P(None, 'tp'), may hold values 0 or 1
- lengths: int32 [2, 4, 2], replicated, may hold values from 1 to 24, 32 in all within a row
- rewards: int32 [2, 4, 2], replicated, may hold values from 0 to 3
- groups: int32 [2, 4, 2], replicated, may hold values from 0 to 7, as said below
- query_weight: bfloat16 [2, 8192, 4096], P('pp', 'fsdp', 'tp'), may hold values from -0.0625 to 0.0625
- key_weight: bfloat16 [2, 8192, 1024], P('pp', 'fsdp', 'tp'), may hold values from -0.0625 to 0.0625
- value_weight: bfloat16 [2, 8192, 1024], P('pp', 'fsdp', 'tp'), may hold values from -1 to 1
- out_weight: bfloat16 [2, 4096, 8192], P('pp', 'tp', 'fsdp'), may hold values from -1 to 1
Outputs:
- query_weight_grad: float32 [2, 8192, 4096], P('pp', 'fsdp', 'tp')
- key_weight_grad: float32 [2, 8192, 1024], P('pp', 'fsdp', 'tp')
- value_weight_grad: float32 [2, 8192, 1024], P('pp', 'fsdp', 'tp')
- out_weight_grad: float32 [2, 4096, 8192], P('pp', 'tp', 'fsdp')
Inputs may be any that keep to these rules, and one draw needn't show every extreme that they name: `groups`: every group value names exactly 2 completions.
All inputs are finite; a program needn't handle non-finite values. No bound on the sum of `noise_mask` on one device may be relied on, other than what follows from the above.
Results may differ from a plain program's by a relative error of at most 0.013.
Values may be sent and summed in bfloat16 or wider, within the bound.
No kernel may reach another device: no remote copies, remote signals or barrier semaphores. Data moves between devices by JAX's collectives and lax.ppermute only.
A program may use at most 128 MiB of HBM per device.

v0:
```python
import jax
import jax.numpy as jnp
from jax import lax
from jax.sharding import PartitionSpec as P

MODEL_WIDTH = 8192
HEAD_WIDTH = 128
SLOT = 32


epsilon = 1e-06
masked_score = -1e30


def from_behind(value, axis, steps):
    count = lax.axis_size(axis)
    initial, last = (max(0, -steps), min(count, count - steps))
    return lax.ppermute(value, axis, [(source, source + steps) for source in range(initial, last)])


def segments(lengths):
    segment_ends = jnp.cumsum(lengths, -1)
    position = jnp.arange(SLOT, dtype=jnp.int32)
    return jnp.sum((segment_ends[..., None, :] <= position[:, None]).astype(jnp.int32), -1)


def token_weights(lengths, rewards, groups):
    group_total = 2 * lengths.shape[1]
    reward_flat = rewards.reshape(-1).astype(jnp.float32)
    member = (
        groups.reshape(-1)[:, None] == jnp.arange(group_total, dtype=jnp.int32)[None, :]
    ).astype(jnp.float32)
    member_count = jnp.sum(member, 0)
    group_mean = jnp.sum(member * reward_flat[:, None], 0) / member_count
    centered = reward_flat - jnp.sum(member * group_mean[None, :], 1)
    variance = jnp.sum(member * (centered * centered)[:, None], 0) / member_count
    spread_own = jnp.sum(member * jnp.sqrt(variance)[None, :], 1)
    advantage = (centered / jnp.maximum(spread_own, 1.0)).reshape(lengths.shape)
    segment = segments(lengths)
    choose = (segment[..., None] == jnp.arange(lengths.shape[2], dtype=jnp.int32)).astype(
        jnp.float32
    )
    token_adv = jnp.sum(choose * advantage[:, :, None, :], -1)
    token_len = jnp.sum(choose * lengths[:, :, None, :].astype(jnp.float32), -1)
    return (token_adv * SLOT / token_len).reshape(lengths.shape[0], -1)


def split_heads(query_rows, key_rows, value_rows):
    batch_count, slot_len = (query_rows.shape[0], query_rows.shape[1])
    kv_heads = key_rows.shape[-1] // HEAD_WIDTH
    group_heads = query_rows.shape[-1] // HEAD_WIDTH // kv_heads
    query_heads = query_rows.reshape(
        batch_count, slot_len, kv_heads, group_heads, HEAD_WIDTH
    ).astype(jnp.float32)
    key_heads = key_rows.reshape(batch_count, slot_len, kv_heads, HEAD_WIDTH).astype(jnp.float32)
    value_heads = value_rows.reshape(batch_count, slot_len, kv_heads, HEAD_WIDTH).astype(
        jnp.float32
    )
    return (query_heads, key_heads, value_heads)


def attend(query_rows, key_rows, value_rows, segment):
    query_heads, key_heads, value_heads = split_heads(query_rows, key_rows, value_rows)
    score_scale = HEAD_WIDTH ** (-0.5)
    scores = jnp.einsum("bikgd,bjkd->bkgij", query_heads, key_heads) * score_scale
    same_doc = segment[:, None, None, :, None] == segment[:, None, None, None, :]
    scores = jnp.where(same_doc, scores, masked_score)
    attn_probs = jax.nn.softmax(scores, axis=-1)
    rounded = lax.optimization_barrier(attn_probs.astype(jnp.bfloat16)).astype(jnp.float32)
    mixture = jnp.einsum("bkgij,bjkd->bikgd", rounded, value_heads)
    return (mixture.reshape(query_rows.shape).astype(jnp.bfloat16), attn_probs)


def attend_back(query_rows, key_rows, value_rows, attn_probs, head_out_grad):
    query_heads, key_heads, value_heads = split_heads(query_rows, key_rows, value_rows)
    score_scale = HEAD_WIDTH ** (-0.5)
    grad_heads = head_out_grad.reshape(query_heads.shape).astype(jnp.float32)
    rounded = lax.optimization_barrier(attn_probs.astype(jnp.bfloat16)).astype(jnp.float32)
    prob_grad = jnp.einsum("bikgd,bjkd->bkgij", grad_heads, value_heads)
    value_grad = jnp.einsum("bkgij,bikgd->bjkd", rounded, grad_heads)
    score_grad = attn_probs * (prob_grad - jnp.sum(prob_grad * attn_probs, -1, keepdims=True))
    score_grad = lax.optimization_barrier(score_grad.astype(jnp.bfloat16)).astype(jnp.float32)
    query_grad = jnp.einsum("bkgij,bjkd->bikgd", score_grad, key_heads) * score_scale
    key_grad = jnp.einsum("bkgij,bikgd->bjkd", score_grad, query_heads) * score_scale
    return (
        query_grad.reshape(query_rows.shape).astype(jnp.bfloat16),
        key_grad.reshape(key_rows.shape).astype(jnp.bfloat16),
        value_grad.reshape(value_rows.shape).astype(jnp.bfloat16),
    )


def front(stream, query_layer, key_layer, value_layer, segment):
    stream_float = stream.astype(jnp.float32)
    squares = lax.psum(jnp.sum(stream_float * stream_float, -1), "fsdp")
    inv_rms = lax.rsqrt(squares / MODEL_WIDTH + epsilon)
    normed = (stream_float * inv_rms[:, None]).astype(jnp.bfloat16)
    normed_all = lax.all_gather(normed, "tp", axis=0, tiled=True)
    query_cols = query_layer.shape[1]
    key_cols = key_layer.shape[1]
    projected = lax.psum_scatter(
        jnp.concatenate(
            [
                jnp.dot(normed_all, query_layer, preferred_element_type=jnp.float32),
                jnp.dot(normed_all, key_layer, preferred_element_type=jnp.float32),
                jnp.dot(normed_all, value_layer, preferred_element_type=jnp.float32),
            ],
            1,
        ),
        "fsdp",
        scatter_dimension=0,
        tiled=True,
    )
    query_rows = projected[:, :query_cols].astype(jnp.bfloat16)
    key_rows = projected[:, query_cols : query_cols + key_cols].astype(jnp.bfloat16)
    value_rows = projected[:, query_cols + key_cols :].astype(jnp.bfloat16)
    head_out, attn_probs = attend(query_rows[None], key_rows[None], value_rows[None], segment)
    return (inv_rms, normed_all, query_rows, key_rows, value_rows, attn_probs, head_out[0])


def spread(head_out):
    return lax.all_gather(head_out, "fsdp", axis=0, tiled=True)


def finish(stream, heads_all, out_layer):
    summed = lax.psum_scatter(
        jnp.dot(heads_all, out_layer, preferred_element_type=jnp.float32),
        "tp",
        scatter_dimension=0,
        tiled=True,
    )
    return (stream.astype(jnp.float32) + summed).astype(jnp.bfloat16)


def back(
    out_grad,
    stream,
    inv_rms,
    normed_all,
    query_rows,
    key_rows,
    value_rows,
    attn_probs,
    heads_all,
    query_layer,
    key_layer,
    value_layer,
    out_layer,
):
    grad_all = lax.all_gather(out_grad, "tp", axis=0, tiled=True)
    out_weight_grad = jnp.einsum(
        "tq,td->qd", heads_all, grad_all, preferred_element_type=jnp.float32
    )
    head_out_grad = lax.psum_scatter(
        jnp.einsum("td,qd->tq", grad_all, out_layer, preferred_element_type=jnp.float32),
        "fsdp",
        scatter_dimension=0,
        tiled=True,
    ).astype(jnp.bfloat16)
    query_grad, key_grad, value_grad = attend_back(
        query_rows[None], key_rows[None], value_rows[None], attn_probs, head_out_grad[None]
    )
    query_all, key_all, value_gathered = (
        lax.all_gather(query_grad[0], "fsdp", axis=0, tiled=True),
        lax.all_gather(key_grad[0], "fsdp", axis=0, tiled=True),
        lax.all_gather(value_grad[0], "fsdp", axis=0, tiled=True),
    )
    query_weight_grad = jnp.einsum(
        "tm,tq->mq", normed_all, query_all, preferred_element_type=jnp.float32
    )
    key_weight_grad = jnp.einsum(
        "tm,tq->mq", normed_all, key_all, preferred_element_type=jnp.float32
    )
    value_weight_grad = jnp.einsum(
        "tm,tq->mq", normed_all, value_gathered, preferred_element_type=jnp.float32
    )
    normed_grad = lax.psum_scatter(
        jnp.einsum("tq,mq->tm", query_all, query_layer, preferred_element_type=jnp.float32)
        + jnp.einsum("tq,mq->tm", key_all, key_layer, preferred_element_type=jnp.float32)
        + jnp.einsum("tq,mq->tm", value_gathered, value_layer, preferred_element_type=jnp.float32),
        "tp",
        scatter_dimension=0,
        tiled=True,
    )
    stream_float = stream.astype(jnp.float32)
    grad_dot = lax.psum(jnp.sum(normed_grad * stream_float, -1), "fsdp")
    input_grad = (
        out_grad.astype(jnp.float32)
        + inv_rms[:, None] * normed_grad
        - stream_float * (inv_rms**3 * grad_dot / MODEL_WIDTH)[:, None]
    ).astype(jnp.bfloat16)
    return (input_grad, (query_weight_grad, key_weight_grad, value_weight_grad, out_weight_grad))


def keep_item(store, index_now, value_now, active):
    return store.at[index_now].set(jnp.where(active, value_now, store[index_now]))


def local(
    inputs,
    head_grad,
    noise_mask,
    lengths,
    rewards,
    groups,
    query_weight,
    key_weight,
    value_weight,
    out_weight,
):
    query_layer, key_layer = (query_weight[0], key_weight[0])
    value_layer, out_layer = (value_weight[0], out_weight[0])
    section_index = lax.axis_index("pp")
    sections = lax.axis_size("pp")
    micro_count, row_count = (inputs.shape[0], inputs.shape[1])
    shard_index = lax.axis_index("fsdp")
    segment_all = segments(lengths)
    weight_all = token_weights(lengths, rewards, groups)
    own_weights = lax.dynamic_slice_in_dim(
        weight_all, lax.axis_index("tp") * row_count, row_count, 1
    ) * noise_mask.astype(jnp.float32)
    top_grad = (-own_weights[:, :, None] * head_grad.astype(jnp.float32)).astype(jnp.bfloat16)
    tick_total = micro_count + sections - 1
    incoming = jnp.zeros_like(inputs[0])
    inputs_kept = jnp.zeros_like(inputs)
    stores = None
    for tick_index in range(tick_total):
        micro_now = tick_index - section_index
        active = (micro_now >= 0) & (micro_now < micro_count)
        slot_micro = jnp.clip(micro_now, 0, micro_count - 1)
        stream = jnp.where(section_index == 0, inputs[min(tick_index, micro_count - 1)], incoming)
        segment = segment_all[slot_micro, shard_index][None]
        inv_rms, normed_all, query_rows, key_rows, value_rows, attn_probs, head_out = front(
            stream, query_layer, key_layer, value_layer, segment
        )
        heads_all = spread(head_out)
        following = finish(stream, heads_all, out_layer)
        inputs_kept = keep_item(inputs_kept, slot_micro, stream, active)
        items = (inv_rms, normed_all, query_rows, key_rows, value_rows, attn_probs, heads_all)
        if stores is None:
            stores = jax.tree.map(
                lambda array_leaf: jnp.zeros((micro_count,) + array_leaf.shape, array_leaf.dtype),
                items,
            )
        stores = jax.tree.map(
            lambda stack_leaf, array_leaf: keep_item(stack_leaf, slot_micro, array_leaf, active),
            stores,
            items,
        )
        if tick_index + 1 < tick_total:
            incoming = from_behind(following, "pp", 1)
    totals = (
        jnp.zeros(query_layer.shape, jnp.float32),
        jnp.zeros(key_layer.shape, jnp.float32),
        jnp.zeros(value_layer.shape, jnp.float32),
        jnp.zeros(out_layer.shape, jnp.float32),
    )
    incoming = jnp.zeros_like(inputs[0])
    for tick_index in range(tick_total):
        micro_now = tick_index - (sections - 1 - section_index)
        active = (micro_now >= 0) & (micro_now < micro_count)
        slot_micro = jnp.clip(micro_now, 0, micro_count - 1)
        out_grad = jnp.where(section_index == sections - 1, top_grad[slot_micro], incoming)
        stream = inputs_kept[slot_micro]
        segment = segment_all[slot_micro, shard_index][None]
        inv_rms, normed_all, query_rows, key_rows, value_rows, attn_probs, heads_all = jax.tree.map(
            lambda stack_leaf: stack_leaf[slot_micro], stores
        )
        input_grad, terms = back(
            out_grad,
            stream,
            inv_rms,
            normed_all,
            query_rows,
            key_rows,
            value_rows,
            attn_probs,
            heads_all,
            query_layer,
            key_layer,
            value_layer,
            out_layer,
        )
        totals = tuple((total + jnp.where(active, term, 0.0) for total, term in zip(totals, terms)))
        if tick_index + 1 < tick_total:
            incoming = from_behind(input_grad, "pp", -1)
    return (totals[0][None], totals[1][None], totals[2][None], totals[3][None])


def solution(mesh):
    return jax.shard_map(
        local,
        mesh=mesh,
        in_specs=(
            P(None, "tp", "fsdp"),
            P(None, "tp", "fsdp"),
            P(None, "tp"),
            P(),
            P(),
            P(),
            P("pp", "fsdp", "tp"),
            P("pp", "fsdp", "tp"),
            P("pp", "fsdp", "tp"),
            P("pp", "tp", "fsdp"),
        ),
        out_specs=(
            P("pp", "fsdp", "tp"),
            P("pp", "fsdp", "tp"),
            P("pp", "fsdp", "tp"),
            P("pp", "tp", "fsdp"),
        ),
        check_vma=False,
    )
```

profile of v0, /device:TPU:0, one launch (start us, length us, event | category | flops | bytes accessed | tf_op | source)
XLA Modules:
  0.0 583.1 jit_solution(12269084936721835985)
XLA Ops:
  8.4 11.4 %psum.35 = f32[32]{0:T(128)S(1)} all-reduce(f32[32]{0:T(128)S(1)} %fusion.124), channel_id=1, replica_groups=mesh['pp'=2,'fsdp'=4,'tp'=4] {'fsdp'}, use_global_device_ids=true, to_apply=%region_2.3 | all-reduce | flops 32 | bytes 256 | tf_op jit(solution)/shard_map/psum | solution.py:94
  23.5 16.0 %all_gather.54 = bf16[128,2048]{1,0:T(8,128)(2,1)S(1)} all-gather(bf16[32,2048]{1,0:T(8,128)(2,1)S(1)} %fusion.125), channel_id=1, replica_groups=mesh['pp'=2,'fsdp'=4,'tp'=4] {'tp'}, dimensions={0}, use_global_device_ids=true | all-gather | bytes 655360 | tf_op jit(solution)/shard_map/all_gather | solution.py:97
  44.1 23.9 %reduce-scatter.11.cloned.1.call-done = f32[32,1536]{1,0:T(8,128)} async-done(((f32[128,1536]{1,0:T(8,128)}), f32[32,1536]{1,0:T(8,128)}) %reduce-scatter.11.cloned.1.call-update) | async-done | bytes 196624 | tf_op jit(solution)/shard_map/reduce_scatter | solution.py:100
  70.2 9.1 %all_gather.55 = bf16[128,1024]{1,0:T(8,128)(2,1)S(1)} all-gather(bf16[32,1024]{1,0:T(8,128)(2,1)S(1)} %convert_element_type.376), channel_id=1, replica_groups=mesh['pp'=2,'fsdp'=4,'tp'=4] {'fsdp'}, dimensions={0}, use_global_device_ids=true | all-gather | bytes 327680 | tf_op jit(solution)/shard_map/all_gather | solution.py:121
  85.9 24.9 %reduce-scatter.13.cloned.1.call-done = f32[32,2048]{1,0:T(8,128)} async-done(((f32[128,2048]{1,0:T(8,128)}), f32[32,2048]{1,0:T(8,128)}) %reduce-scatter.13.cloned.1.call-update) | async-done | bytes 262160 | tf_op jit(solution)/shard_map/reduce_scatter | solution.py:125
  114.9 9.8 %psum.36 = f32[32]{0:T(128)S(1)} all-reduce(f32[32]{0:T(128)S(1)} %fusion.121), channel_id=1, replica_groups=mesh['pp'=2,'fsdp'=4,'tp'=4] {'fsdp'}, use_global_device_ids=true, to_apply=%region_11.12 | all-reduce | flops 32 | bytes 256 | tf_op jit(solution)/shard_map/psum | solution.py:94
  125.4 15.6 %all_gather.56 = bf16[128,2048]{1,0:T(8,128)(2,1)S(1)} all-gather(bf16[32,2048]{1,0:T(8,128)(2,1)S(1)} %fusion.122), channel_id=1, replica_groups=mesh['pp'=2,'fsdp'=4,'tp'=4] {'tp'}, dimensions={0}, use_global_device_ids=true | all-gather | bytes 655360 | tf_op jit(solution)/shard_map/all_gather | solution.py:97
  146.1 15.2 %all-gather = bf16[1,128,2048]{2,1,0:T(8,128)(2,1)S(1)} all-gather(bf16[1,32,2048]{2,1,0:T(8,128)(2,1)S(1)} %dynamic-slice_select_fusion), channel_id=2, replica_groups=mesh['pp'=2,'fsdp'=4,'tp'=4] {'tp'}, dimensions={1}, use_global_device_ids=true | all-gather | bytes 655360 | tf_op jit(solution)/shard_map/all_gather | solution.py:149
  184.6 10.4 %reduce-scatter.21.cloned.1.call-done = f32[32,1024]{1,0:T(8,128)} async-done(((f32[128,1024]{1,0:T(8,128)}), f32[32,1024]{1,0:T(8,128)}) %reduce-scatter.21.cloned.1.call-update) | async-done | bytes 131088 | tf_op jit(solution)/shard_map/reduce_scatter | solution.py:153
  202.4 22.7 %reduce-scatter.17.cloned.1.call-done = f32[32,2048]{1,0:T(8,128)} async-done(((f32[128,2048]{1,0:T(8,128)}), f32[32,2048]{1,0:T(8,128)}) %reduce-scatter.17.cloned.1.call-update) | async-done | bytes 262160 | tf_op jit(solution)/shard_map/reduce_scatter | solution.py:125
  229.3 9.8 %psum.37 = f32[32]{0:T(128)S(1)} all-reduce(f32[32]{0:T(128)S(1)} %fusion.113), channel_id=1, replica_groups=mesh['pp'=2,'fsdp'=4,'tp'=4] {'fsdp'}, use_global_device_ids=true, to_apply=%region_18.19 | all-reduce | flops 32 | bytes 256 | tf_op jit(solution)/shard_map/psum | solution.py:94
  239.7 15.7 %all_gather.58 = bf16[128,2048]{1,0:T(8,128)(2,1)S(1)} all-gather(bf16[32,2048]{1,0:T(8,128)(2,1)S(1)} %fusion.114), channel_id=1, replica_groups=mesh['pp'=2,'fsdp'=4,'tp'=4] {'tp'}, dimensions={0}, use_global_device_ids=true | all-gather | bytes 655360 | tf_op jit(solution)/shard_map/all_gather | solution.py:97
  264.9 16.2 %reduce-scatter.19.cloned.1.call-done = f32[32,1536]{1,0:T(8,128)} async-done(((f32[128,1536]{1,0:T(8,128)}), f32[32,1536]{1,0:T(8,128)}) %reduce-scatter.19.cloned.1.call-update) | async-done | bytes 196624 | tf_op jit(solution)/shard_map/reduce_scatter | solution.py:100
  291.5 8.5 %all_gather.61 = bf16[128,256]{1,0:T(8,128)(2,1)S(1)} all-gather(bf16[32,256]{1,0:T(8,128)(2,1)S(1)} %bitcast.544), channel_id=1, replica_groups=mesh['pp'=2,'fsdp'=4,'tp'=4] {'fsdp'}, dimensions={0}, use_global_device_ids=true | all-gather | bytes 81920 | tf_op jit(solution)/shard_map/all_gather | solution.py:164
  332.2 16.2 %reduce-scatter.23.cloned.1.call-done = f32[32,2048]{1,0:T(8,128)} async-done(((f32[128,2048]{1,0:T(8,128)}), f32[32,2048]{1,0:T(8,128)}) %reduce-scatter.23.cloned.1.call-update) | async-done | bytes 262160 | tf_op jit(solution)/shard_map/reduce_scatter | solution.py:176
  349.5 10.3 %psum.38 = f32[32]{0:T(128)} all-reduce(f32[32]{0:T(128)S(1)} %fusion.115), channel_id=1, replica_groups=mesh['pp'=2,'fsdp'=4,'tp'=4] {'fsdp'}, use_global_device_ids=true, to_apply=%region_39.40 | all-reduce | flops 32 | bytes 256 | tf_op jit(solution)/shard_map/psum | solution.py:185
  368.7 16.1 %all_gather.63 = bf16[128,2048]{1,0:T(8,128)(2,1)S(1)} all-gather(bf16[32,2048]{1,0:T(8,128)(2,1)S(1)} %bitcast_select_fusion.13), channel_id=1, replica_groups=mesh['pp'=2,'fsdp'=4,'tp'=4] {'tp'}, dimensions={0}, use_global_device_ids=true | all-gather | bytes 655360 | tf_op jit(solution)/shard_map/all_gather | solution.py:149
  398.6 8.7 %all_gather.71 = bf16[128,1024]{1,0:T(8,128)(2,1)} all-gather(bf16[32,1024]{1,0:T(8,128)(2,1)S(1)} %convert_element_type.452), channel_id=1, replica_groups=mesh['pp'=2,'fsdp'=4,'tp'=4] {'fsdp'}, dimensions={0}, use_global_device_ids=true | all-gather | bytes 327680 | tf_op jit(solution)/shard_map/all_gather | solution.py:121
  436.4 8.8 %all_gather.64 = bf16[128,1024]{1,0:T(8,128)(2,1)S(1)} all-gather(bf16[32,1024]{1,0:T(8,128)(2,1)} %convert_element_type.419), channel_id=1, replica_groups=mesh['pp'=2,'fsdp'=4,'tp'=4] {'fsdp'}, dimensions={0}, use_global_device_ids=true | all-gather | bytes 327680 | tf_op jit(solution)/shard_map/all_gather | solution.py:163
  477.3 9.8 %psum.39 = f32[32]{0:T(128)S(1)} all-reduce(f32[32]{0:T(128)S(1)} %fusion.118), channel_id=1, replica_groups=mesh['pp'=2,'fsdp'=4,'tp'=4] {'fsdp'}, use_global_device_ids=true, to_apply=%region_44.45 | all-reduce | flops 32 | bytes 256 | tf_op jit(solution)/shard_map/psum | solution.py:185
  493.3 16.1 %all_gather.67 = bf16[128,2048]{1,0:T(8,128)(2,1)S(1)} all-gather(bf16[32,2048]{1,0:T(8,128)(2,1)S(1)} %bitcast_select_fusion.8), channel_id=1, replica_groups=mesh['pp'=2,'fsdp'=4,'tp'=4] {'tp'}, dimensions={0}, use_global_device_ids=true | all-gather | bytes 655360 | tf_op jit(solution)/shard_map/all_gather | solution.py:149
  523.6 10.2 %reduce-scatter.29.cloned.1.call-done = f32[32,1024]{1,0:T(8,128)} async-done(((f32[128,1024]{1,0:T(8,128)}), f32[32,1024]{1,0:T(8,128)}) %reduce-scatter.29.cloned.1.call-update) | async-done | bytes 131088 | tf_op jit(solution)/shard_map/reduce_scatter | solution.py:153
  551.7 9.2 %all_gather.68 = bf16[128,1024]{1,0:T(8,128)(2,1)S(1)} all-gather(bf16[32,1024]{1,0:T(8,128)(2,1)S(1)} %convert_element_type.438), channel_id=1, replica_groups=mesh['pp'=2,'fsdp'=4,'tp'=4] {'fsdp'}, dimensions={0}, use_global_device_ids=true | all-gather | bytes 327680 | tf_op jit(solution)/shard_map/all_gather | solution.py:163
  567.7 8.5 %add_bitcast_fusion.1 = f32[1,2048,1024]{2,1,0:T(8,128)} fusion(f32[2048,1024]{1,0:T(8,128)} %fusion.93, f32[2048,1024]{1,0:T(8,128)} %fusion.100, bf16[128,1024]{1,0:T(8,128)(2,1)S(1)} %all_gather.68, pred[]{:T(512)S(6)} %and.134, pred[]{:T(512)S(6)} %and.130, pred[]{:T(512)S(6)} %and.120, bf16[2,128,2048]{2,1,0:T(8,128)(2,1)S(1)} %fusion.102, s32[]{:T(128)S(6)} %min.33), kind=kOutput, calls=%fused_computation.1 | convolution fusion | flops 547356672 | bytes 25952264 | tf_op jit(solution)/shard_map/tm,tq->mq/dot_general | solution.py:167
  (385 shorter events, 244.6 us)
Async XLA Ops:
  7.2 34.1 %copy-start = (bf16[1,2048,256]{2,1,0:T(8,128)(2,1)S(1)}, bf16[1,2048,256]{2,1,0:T(8,128)(2,1)}, u32[]{:S(2)}) copy-start(bf16[1,2048,256]{2,1,0:T(8,128)(2,1)} %param.65) | copy-start | bytes 3145732
  7.2 60.8 %reduce-scatter.11.cloned.1.call-start = ((), (), s32[]{:S(2)}) async-start(), calls=%async_computation.10 | async-start | bytes 983040 | tf_op jit(solution)/shard_map/reduce_scatter | solution.py:100
  43.3 67.5 %reduce-scatter.13.cloned.1.call-start = ((), (), s32[]{:S(2)}) async-start(), calls=%async_computation.11 | async-start | bytes 1310720 | tf_op jit(solution)/shard_map/reduce_scatter | solution.py:125
  79.3 35.5 %copy-start.23 = (bf16[128,1024]{1,0:T(8,128)(2,1)}, bf16[128,1024]{1,0:T(8,128)(2,1)S(1)}, u32[]{:S(2)}) copy-start(bf16[128,1024]{1,0:T(8,128)(2,1)S(1)} %all_gather.55) | copy-start | bytes 786436
  79.3 61.7 %copy-start.8 = (bf16[1,2048,256]{2,1,0:T(8,128)(2,1)S(1)}, bf16[1,2048,256]{2,1,0:T(8,128)(2,1)}, u32[]{:S(2)}) copy-start(bf16[1,2048,256]{2,1,0:T(8,128)(2,1)} %param.66) | copy-start | bytes 3145732
  83.3 84.0 %reduce-scatter.15.cloned.1.call-start = ((), (), s32[]{:S(2)}) async-start(), calls=%async_computation.12 | async-start | bytes 983040 | tf_op jit(solution)/shard_map/reduce_scatter | solution.py:100
  111.7 2.3 collective-permute-start
  143.4 51.7 %reduce-scatter.21.cloned.1.call-start = ((), (), s32[]{:S(2)}) async-start(), calls=%async_computation.15 | async-start | bytes 655360 | tf_op jit(solution)/shard_map/reduce_scatter | solution.py:153
  146.0 32.2 %copy-start.21 = (bf16[2,32,2048]{2,1,0:T(8,128)(2,1)}, bf16[2,32,2048]{2,1,0:T(8,128)(2,1)S(1)}, u32[]{:S(2)}) copy-start(bf16[2,32,2048]{2,1,0:T(8,128)(2,1)S(1)} %multiply_convert_fusion) | copy-start | bytes 786436
  166.6 58.5 %reduce-scatter.17.cloned.1.call-start = ((), (), s32[]{:S(2)}) async-start(), calls=%async_computation.13 | async-start | bytes 1310720 | tf_op jit(solution)/shard_map/reduce_scatter | solution.py:125
  178.2 50.9 %copy-start.24 = (bf16[128,1024]{1,0:T(8,128)(2,1)}, bf16[128,1024]{1,0:T(8,128)(2,1)S(1)}, u32[]{:S(2)}) copy-start(bf16[128,1024]{1,0:T(8,128)(2,1)S(1)} %all_gather.57) | copy-start | bytes 786436
  182.3 98.8 %reduce-scatter.19.cloned.1.call-start = ((), (), s32[]{:S(2)}) async-start(), calls=%async_computation.14 | async-start | bytes 983040 | tf_op jit(solution)/shard_map/reduce_scatter | solution.py:100
  202.4 56.1 %copy-start.31 = (bf16[2,32,1024]{2,1,0:T(8,128)(2,1)}, bf16[2,32,1024]{2,1,0:T(8,128)(2,1)S(1)}, u32[]{:S(2)}) copy-start(bf16[2,32,1024]{2,1,0:T(8,128)(2,1)S(1)} %bitcast_dynamic-update-slice_fusion.3) | copy-start | bytes 393220
  226.1 2.3 collective-permute-start.1
  257.7 31.1 %copy-start.50 = (pred[32,32]{0,1:T(8,128)(4,1)S(1)}, pred[32,32]{0,1:T(8,128)(4,1)}, u32[]{:S(2)}) copy-start(pred[32,32]{0,1:T(8,128)(4,1)} %get-tuple-element.354) | copy-start | bytes 3076
  257.7 32.8 %copy-start.42 = (bf16[32,2,4,128]{3,2,1,0:T(4,128)(2,1)S(1)}, bf16[32,2,4,128]{3,2,1,0:T(4,128)(2,1)}, u32[]{:S(2)}) copy-start(bf16[32,2,4,128]{3,2,1,0:T(4,128)(2,1)} %reshape.1304) | copy-start | bytes 196612
  257.8 90.6 %reduce-scatter.23.cloned.1.call-start = ((), (), s32[]{:S(2)}) async-start(), calls=%async_computation.16 | async-start | bytes 1310720 | tf_op jit(solution)/shard_map/reduce_scatter | solution.py:176
  320.9 91.5 %reduce-scatter.25.cloned.1.call-start = ((), (), s32[]{:S(2)}) async-start(), calls=%async_computation.17 | async-start | bytes 655360 | tf_op jit(solution)/shard_map/reduce_scatter | solution.py:153
  332.2 58.0 %copy-start.56 = (f32[2,32]{1,0:T(2,128)}, f32[2,32]{1,0:T(2,128)S(1)}, u32[]{:S(2)}) copy-start(f32[2,32]{1,0:T(2,128)S(1)} %scatter.104) | copy-start | bytes 772
  361.7 5.5 collective-permute-start.2
  390.2 86.1 %reduce-scatter.27.cloned.1.call-start = ((), (), s32[]{:S(2)}) async-start(), calls=%async_computation.18 | async-start | bytes 1310720 | tf_op jit(solution)/shard_map/reduce_scatter | solution.py:176
  396.1 29.5 %copy-start.49 = (bf16[32,2,128]{2,1,0:T(2,128)(2,1)S(1)}, bf16[32,2,128]{2,1,0:T(2,128)(2,1)}, u32[]{:S(2)}) copy-start(bf16[32,2,128]{2,1,0:T(2,128)(2,1)} %reshape.1306) | copy-start | bytes 49156
  448.8 85.0 %reduce-scatter.29.cloned.1.call-start = ((), (), s32[]{:S(2)}) async-start(), calls=%async_computation.19 | async-start | bytes 655360 | tf_op jit(solution)/shard_map/reduce_scatter | solution.py:153
  488.4 4.9 collective-permute-start.3
  (53 other events, 510.4 us)
Sparse Core Ops, SparseCore 0:
  43.4 24.4 reduce-scatter.10
  83.5 27.2 reduce-scatter.12
  143.5 23.1 reduce-scatter.14
  169.9 25.1 reduce-scatter.20
  197.8 27.2 reduce-scatter.16
  257.9 23.1 reduce-scatter.18
  321.0 27.2 reduce-scatter.22
  390.3 22.0 reduce-scatter.24
  448.9 27.2 reduce-scatter.26
  511.9 21.8 reduce-scatter.28
where the time goes:
time: 586 us; the launch traced here: 583 us
  blocking collectives  246 us (42%)
  waiting for transfers between devices  134 us (23%)
  matrix products  93.6 us (16%)
  other arithmetic  56.1 us (10%)
  local copies, waits for them, and re-layouts  31.5 us (5%)
  between operations  15.5 us (3%)
  starting transfers between devices  6.07 us (1%)
    reduce_scatter x2, waiting for transfers between devices, finish(): lax.psum_scatter(jnp.dot(heads_all, out_layer, preferred_element_type=jnp...  47.5 us
    all_gather x3, blocking collectives, back(): grad_all = lax.all_gather(out_grad, 'tp', axis=0, tiled=True)  47.4 us
    all_gather x3, blocking collectives, front(): normed_all = lax.all_gather(normed, 'tp', axis=0, tiled=True)  47.2 us
    reduce_scatter x3, waiting for transfers between devices, front(): lax.psum_scatter(jnp.concatenate([jnp.dot(normed_all, query_layer, prefer...  40 us
    psum x3, blocking collectives, front(): squares = lax.psum(jnp.sum(stream_float * stream_float, -1), 'fsdp')  31 us
    all_gather x3, blocking collectives, spread(): return lax.all_gather(head_out, 'fsdp', axis=0, tiled=True)  26 us
    all_gather x3, blocking collectives, back(): lax.all_gather(query_grad[0], 'fsdp', axis=0, tiled=True)  26 us
    all_gather x3, blocking collectives, back(): lax.all_gather(value_grad[0], 'fsdp', axis=0, tiled=True)  24.9 us
  transfers between devices with their start and end apart: 14, of which 11 were waited for; matrix products, arithmetic and copies ran while one was open for 17% of the time, Pallas kernels for 0%

commit v1 on v0

v1 whole, which is shorter than its diff:
```python
import functools

import jax
import jax.numpy as jnp
from jax import lax
from jax.experimental import pallas as pl
from jax.experimental.pallas import tpu as pltpu
from jax.sharding import PartitionSpec as P

MODEL_WIDTH = 8192
HEAD_WIDTH = 128
SLOT = 32
LANES = 128
BLOCK = 128

epsilon = 1e-06
masked_score = -1e30
bf16 = jnp.bfloat16
f32 = jnp.float32


def segments(lengths):
    segment_ends = jnp.cumsum(lengths, -1)
    position = jnp.arange(SLOT, dtype=jnp.int32)
    return jnp.sum((segment_ends[..., None, :] <= position[:, None]).astype(jnp.int32), -1)


def token_weights(lengths, rewards, groups, segment):
    group_total = 2 * lengths.shape[1]
    reward_flat = rewards.reshape(-1).astype(f32)
    member = (
        groups.reshape(-1)[:, None] == jnp.arange(group_total, dtype=jnp.int32)[None, :]
    ).astype(f32)
    member_count = jnp.sum(member, 0)
    group_mean = jnp.sum(member * reward_flat[:, None], 0) / member_count
    centered = reward_flat - jnp.sum(member * group_mean[None, :], 1)
    variance = jnp.sum(member * (centered * centered)[:, None], 0) / member_count
    spread_own = jnp.sum(member * jnp.sqrt(variance)[None, :], 1)
    advantage = (centered / jnp.maximum(spread_own, 1.0)).reshape(lengths.shape)
    choose = (segment[..., None] == jnp.arange(lengths.shape[2], dtype=jnp.int32)).astype(f32)
    token_adv = jnp.sum(choose * advantage[:, :, None, :], -1)
    token_len = jnp.sum(choose * lengths[:, :, None, :].astype(f32), -1)
    return (token_adv * SLOT / token_len).reshape(lengths.shape[0], -1)


def exchange(value, axis, bit):
    count = lax.axis_size(axis)
    return lax.ppermute(value, axis, [(source, source ^ bit) for source in range(count)])


def call(body, outs, args, smem=(), hbm=(), scratch=(), flops=0):
    def spec(place):
        space = pltpu.SMEM if place in smem else pl.ANY if place in hbm else pltpu.VMEM
        return pl.BlockSpec(memory_space=space)

    moved = sum(a.size * a.dtype.itemsize for a in args) + sum(
        o.size * o.dtype.itemsize for o in outs
    )
    result = pl.pallas_call(
        body,
        out_shape=list(outs),
        in_specs=[spec(place) for place in range(len(args))],
        out_specs=[pl.BlockSpec(memory_space=pltpu.VMEM)] * len(outs),
        scratch_shapes=list(scratch),
        cost_estimate=pl.CostEstimate(flops=flops, bytes_accessed=moved, transcendentals=0),
    )(*args)
    return result


def shape(rows, columns, kind):
    return jax.ShapeDtypeStruct((rows, columns), kind)


def lane_of(rows):
    return lax.broadcasted_iota(jnp.int32, (rows, LANES), 1)


def first_lane(total):
    return jnp.where(lane_of(total.shape[0]) == 0, total, 0.0)


def high_low(total):
    high = total.astype(bf16).astype(f32)
    lane = lane_of(total.shape[0])
    return jnp.where(lane == 0, high, jnp.where(lane == 1, total - high, 0.0)).astype(bf16)


def fetch(core, layer, own, other, target, sem):
    rows = target.shape[0]
    mine = own.at[pl.ds(pl.multiple_of(core * rows, rows), rows), :]

    @pl.when(core == layer)
    def _():
        pltpu.make_async_copy(mine, target, sem).start()

    @pl.when(core != layer)
    def _():
        pltpu.make_async_copy(other, target, sem).start()

    return pltpu.make_async_copy(other, target, sem)


def part(index, size):
    return pl.ds(pl.multiple_of(index * size, LANES), size)


def project_kernel(
    layer, core_ref, x_ref, qo, ko, vo, qr, kr, vr, keep, send, wq, wk, wv, sems
):
    core = core_ref[0]
    waits = [
        fetch(core, layer, own, other, target, sems.at[place])
        for place, (own, other, target) in enumerate(((qo, qr, wq), (ko, kr, wk), (vo, vr, wv)))
    ]
    x = x_ref[...]
    wide = x.astype(f32)
    squares = jnp.sum(wide * wide, -1, keepdims=True)
    start = 0
    for weight, wait in zip((wq, wk, wv), waits):
        wait.wait()
        half = weight.shape[1] // 2
        keep[:, start : start + half] = jnp.dot(
            x, weight[:, part(core, half)], preferred_element_type=f32
        )
        send[:, start : start + half] = jnp.dot(
            x, weight[:, part(1 - core, half)], preferred_element_type=f32
        ).astype(bf16)
        start += half
    keep[:, start:] = first_lane(squares)
    send[:, start:] = high_low(squares)


def add_kernel(tail, counts, keep, *refs):
    recvs, out, sends = refs[: counts[0]], refs[counts[0]], refs[counts[0] + 1 :]
    columns = keep.shape[1] - (LANES if tail else 0)
    rows = keep.shape[0] // len(recvs)
    for place, recv in enumerate(recvs):
        span = slice(place * rows, (place + 1) * rows)
        out[span, :columns] = keep[span, :columns] + recv[:, :columns].astype(f32)
        if tail:
            total = jnp.sum(
                keep[span, columns:] + recv[:, columns:].astype(f32), -1, keepdims=True
            )
            out[span, columns:] = first_lane(total)
    if sends:
        rows = keep.shape[0] // len(sends)
        for place, send in enumerate(sends):
            span = slice(place * rows, (place + 1) * rows)
            send[:, :columns] = out[span, :columns].astype(bf16)
            if tail:
                send[:, columns:] = high_low(jnp.sum(out[span, columns:], -1, keepdims=True))


def add(keep, recvs, sends, tail):
    rows, columns = keep.shape
    outs = [shape(rows, columns, f32)] + [shape(rows // sends, columns, bf16)] * sends
    body = functools.partial(add_kernel, tail, (len(recvs), sends))
    return call(body, outs, [keep, *recvs])


def sum_fsdp(keep, sends, tail):
    bits = [1 << place for place in range(lax.axis_size("fsdp").bit_length() - 1)]
    middle = len(bits) // 2
    orders = (bits, bits[middle:] + bits[:middle])
    for place in range(len(bits)):
        recvs = [exchange(send, "fsdp", order[place]) for send, order in zip(sends, orders)]
        if place + 1 < len(bits):
            keep, *sends = add(keep, recvs, 2, tail)
    return keep, recvs


def attend(rows_ref, seg_col, seg_row, block, head, kv_place, group):
    span = slice(block * BLOCK, (block + 1) * BLOCK)
    heads_q = rows_ref.shape[1] // HEAD_WIDTH * group // (group + 2)
    kv_heads = heads_q // group
    query = rows_ref[span, head * HEAD_WIDTH : (head + 1) * HEAD_WIDTH]
    key_at = (heads_q + kv_place) * HEAD_WIDTH
    value_at = key_at + kv_heads * HEAD_WIDTH
    key = rows_ref[span, key_at : key_at + HEAD_WIDTH]
    value = rows_ref[span, value_at : value_at + HEAD_WIDTH]
    scores = lax.dot_general(
        query, key, (((1,), (1,)), ((), ())), preferred_element_type=f32
    ) * HEAD_WIDTH ** (-0.5)
    same = seg_col[span, :] == seg_row[0:1, span]
    scores = jnp.where(same, scores, masked_score)
    powers = jnp.exp(scores - jnp.max(scores, -1, keepdims=True))
    probs = powers / jnp.sum(powers, -1, keepdims=True)
    return span, query, key, value, probs


def attend_back(span, query, key, value, probs, rounded, grad):
    scale = HEAD_WIDTH ** (-0.5)
    prob_grad = lax.dot_general(
        grad, value, (((1,), (1,)), ((), ())), preferred_element_type=f32
    )
    value_grad = lax.dot_general(
        rounded, grad, (((0,), (0,)), ((), ())), preferred_element_type=f32
    )
    score_grad = probs * (prob_grad - jnp.sum(prob_grad * probs, -1, keepdims=True))
    score_grad = score_grad.astype(bf16)
    query_grad = jnp.dot(score_grad, key, preferred_element_type=f32) * scale
    key_grad = (
        lax.dot_general(score_grad, query, (((0,), (0,)), ((), ())), preferred_element_type=f32)
        * scale
    )
    return query_grad, key_grad, value_grad


def totals(keep, recvs, columns, span_rows):
    rows = keep.shape[0] // len(recvs)
    for place, recv in enumerate(recvs):
        yield slice(place * rows, (place + 1) * rows), recv


def make_rows(keep, recvs, rows_out, inv_out, raw):
    columns = rows_out.shape[1]
    height = keep.shape[0] // len(recvs)
    for place, recv in enumerate(recvs):
        span = slice(place * height, (place + 1) * height)
        total = keep[span, :columns] + recv[:, :columns].astype(f32)
        squares = jnp.sum(keep[span, columns:] + recv[:, columns:].astype(f32), -1, keepdims=True)
        inv_rms = lax.rsqrt(squares / MODEL_WIDTH + epsilon)
        inv_out[span, :] = jnp.broadcast_to(inv_rms, (height, LANES))
        rows_out[span, :] = (total * inv_rms).astype(bf16)
        if raw is not None:
            raw[span, :] = total


def forward_kernel(group, keep, recv_a, recv_b, seg_col, seg_row, rows_out, inv_out, heads_out):
    make_rows(keep, (recv_a, recv_b), rows_out, inv_out, None)
    heads = heads_out.shape[1] // HEAD_WIDTH
    for block in range(keep.shape[0] // BLOCK):
        for head in range(heads):
            span, _, _, value, probs = attend(
                rows_out, seg_col, seg_row, block, head, head // group, group
            )
            heads_out[span, head * HEAD_WIDTH : (head + 1) * HEAD_WIDTH] = jnp.dot(
                probs.astype(bf16), value, preferred_element_type=f32
            ).astype(bf16)


def back_blocks(group, rows_ref, seg_col, seg_row, grad_of, grads_out, heads_out):
    heads = rows_ref.shape[1] // HEAD_WIDTH * group // (group + 2)
    kv_heads = heads // group
    for block in range(rows_ref.shape[0] // BLOCK):
        for kv_place in range(kv_heads):
            key_sum = value_sum = None
            for head in range(kv_place * group, (kv_place + 1) * group):
                span, query, key, value, probs = attend(
                    rows_ref, seg_col, seg_row, block, head, kv_place, group
                )
                rounded = probs.astype(bf16)
                here = slice(head * HEAD_WIDTH, (head + 1) * HEAD_WIDTH)
                if heads_out is not None:
                    heads_out[span, here] = jnp.dot(
                        rounded, value, preferred_element_type=f32
                    ).astype(bf16)
                query_grad, key_grad, value_grad = attend_back(
                    span, query, key, value, probs, rounded, grad_of(span, here)
                )
                grads_out[span, here] = query_grad.astype(bf16)
                key_sum = key_grad if key_sum is None else key_sum + key_grad
                value_sum = value_grad if value_sum is None else value_sum + value_grad
            at = (heads + kv_place) * HEAD_WIDTH
            grads_out[span, at : at + HEAD_WIDTH] = key_sum.astype(bf16)
            at = at + kv_heads * HEAD_WIDTH
            grads_out[span, at : at + HEAD_WIDTH] = value_sum.astype(bf16)


def sum_grad(keep, recvs, target):
    height = keep.shape[0] // len(recvs)
    for place, recv in enumerate(recvs):
        span = slice(place * height, (place + 1) * height)
        target[span, :] = (keep[span, :] + recv[...].astype(f32)).astype(bf16)


def both_kernel(
    group, keep, recv_a, recv_b, grad_keep, grad_a, grad_b, seg_col, seg_row,
    inv_out, heads_out, grads_out, dots_out, rows, raw, grad,
):
    make_rows(keep, (recv_a, recv_b), rows, inv_out, raw)
    sum_grad(grad_keep, (grad_a, grad_b), grad)
    columns = rows.shape[1]
    back_blocks(
        group, rows, seg_col, seg_row, lambda span, here: grad[span, here], grads_out, heads_out
    )
    dots = jnp.sum(grads_out[:, :columns].astype(f32) * raw[...], -1, keepdims=True)
    dots_out[...] = first_lane(dots)
    grads_out[:, columns:] = high_low(dots)


def back_kernel(group, rows, grad_keep, grad_a, grad_b, seg_col, seg_row, grads_out, grad):
    sum_grad(grad_keep, (grad_a, grad_b), grad)
    back_blocks(
        group, rows, seg_col, seg_row, lambda span, here: grad[span, here], grads_out, None
    )


def out_kernel(layer, core_ref, heads, own, other, keep, send, weight, sem):
    core = core_ref[0]
    fetch(core, layer, own, other, weight, sem).wait()
    half = weight.shape[1] // 2
    keep[...] = jnp.dot(heads[...], weight[:, part(core, half)], preferred_element_type=f32)
    send[...] = jnp.dot(
        heads[...], weight[:, part(1 - core, half)], preferred_element_type=f32
    ).astype(bf16)


def halve_kernel(keep, recv, out, send):
    half = keep.shape[0] // 2
    out[...] = keep[:half, :] + recv[:half, :].astype(f32)
    send[...] = (keep[half:, :] + recv[half:, :].astype(f32)).astype(bf16)


def stream_kernel(keep, recv, stream, out):
    quarter = keep.shape[0] // 2
    for place in range(2):
        span = slice(place * quarter, (place + 1) * quarter)
        back = slice((1 - place) * quarter, (2 - place) * quarter)
        total = keep[span, :] + recv[back, :].astype(f32)
        out[span, :] = (stream[span, :].astype(f32) + total).astype(bf16)


def grad_kernel(keep, recv, grad, stream, inv_ref, out):
    quarter = keep.shape[0] // 2
    columns = out.shape[1]
    for place in range(2):
        span = slice(place * quarter, (place + 1) * quarter)
        back = slice((1 - place) * quarter, (2 - place) * quarter)
        total = keep[span, :columns] + recv[back, :columns].astype(f32)
        dots = jnp.sum(keep[span, columns:] + recv[back, columns:].astype(f32), -1, keepdims=True)
        inv_rms = inv_ref[span, 0:1]
        out[span, :] = (
            grad[span, :].astype(f32)
            + inv_rms * total
            - stream[span, :].astype(f32) * (inv_rms * inv_rms * inv_rms * dots / MODEL_WIDTH)
        ).astype(bf16)


def heads_kernel(layer, core_ref, own_grad, other_grad, own, other, keep, *rest):
    sends, (weight, sem) = rest[:-2], rest[-2:]
    core = core_ref[0]
    fetch(core, layer, own, other, weight, sem).wait()
    half = weight.shape[1] // 2
    turned = (((1,), (1,)), ((), ()))
    keep[...] = lax.dot_general(
        own_grad[...], weight[:, part(core, half)], turned, preferred_element_type=f32
    ) + lax.dot_general(
        other_grad[...], weight[:, part(1 - core, half)], turned, preferred_element_type=f32
    )
    rows = keep.shape[0] // len(sends)
    for place, send in enumerate(sends):
        send[...] = keep[place * rows : (place + 1) * rows, :].astype(bf16)


def normed_kernel(
    layer, core_ref, own_grads, other_grads, dots, qo, ko, vo, qr, kr, vr,
    keep, send, wq, wk, wv, total, sems,
):
    core = core_ref[0]
    waits = [
        fetch(core, layer, own, other, target, sems.at[place])
        for place, (own, other, target) in enumerate(((qo, qr, wq), (ko, kr, wk), (vo, vr, wv)))
    ]
    turned = (((1,), (1,)), ((), ()))
    start = 0
    for weight, wait in zip((wq, wk, wv), waits):
        wait.wait()
        half = weight.shape[1] // 2
        term = lax.dot_general(
            own_grads[:, start : start + half], weight[:, part(core, half)], turned,
            preferred_element_type=f32,
        ) + lax.dot_general(
            other_grads[:, start : start + half], weight[:, part(1 - core, half)], turned,
            preferred_element_type=f32,
        )
        total[...] = term if start == 0 else total[...] + term
        start += half
    half = total.shape[0] // 2
    columns = total.shape[1]
    dot_total = jnp.sum(dots[...] + other_grads[:, start:].astype(f32), -1, keepdims=True)
    keep[:, :columns] = total[:half, :]
    keep[:, columns:] = first_lane(dot_total[:half])
    send[:, :columns] = total[half:, :].astype(bf16)
    send[:, columns:] = high_low(dot_total[half:])


def gather_tokens(own):
    near, far, cross = (exchange(own, "tp", bit) for bit in (1, 2, 3))
    return jnp.concatenate([own, far, near, cross])


def local(
    inputs, head_grad, noise_mask, lengths, rewards, groups,
    query_weight, key_weight, value_weight, out_weight,
):
    core = lax.axis_index("pp")
    shard = lax.axis_index("tp")
    micro, own_rows, features = inputs.shape
    half = features // 2
    piece = micro * own_rows
    rows = 4 * piece
    own = [query_weight[0], key_weight[0], value_weight[0], out_weight[0]]
    group = own[0].shape[1] // own[1].shape[1]
    head_cols = own[0].shape[1] // 2
    kv_cols = own[1].shape[1] // 2
    columns = head_cols + 2 * kv_cols
    core_vec = core.astype(jnp.int32)[None]

    own_inputs = lax.dynamic_slice_in_dim(inputs, core * half, half, 2).reshape(piece, half)
    stream0 = gather_tokens(own_inputs)

    def swap(value):
        return exchange(value, "pp", 1)

    other = [
        swap(lax.dynamic_slice_in_dim(w, (1 - core) * (w.shape[0] // 2), w.shape[0] // 2, 0))
        for w in own
    ]

    segment = segments(lengths)
    weight_all = token_weights(lengths, rewards, groups, segment)
    own_weights = lax.dynamic_slice_in_dim(
        weight_all, shard * own_rows, own_rows, 1
    ) * noise_mask.astype(f32)
    own_head = lax.dynamic_slice_in_dim(head_grad, core * half, half, 2)
    top_grad = (-own_weights[:, :, None] * own_head.astype(f32)).astype(bf16).reshape(piece, half)

    slots = segment.shape[1]
    named = segment + lengths.shape[2] * (
        jnp.arange(micro, dtype=jnp.int32)[:, None, None] * slots
        + jnp.arange(slots, dtype=jnp.int32)[None, :, None]
    )
    named = jnp.swapaxes(named.reshape(micro, 4, own_rows), 0, 1).reshape(4, piece)
    order = shard ^ jnp.array([0, 2, 1, 3], jnp.int32)
    pick = (order[:, None] == jnp.arange(4, dtype=jnp.int32)[None, :]).astype(jnp.int32)
    named = jnp.sum(pick[:, :, None] * named[None], 1).reshape(rows)
    seg_col = jnp.broadcast_to(named[:, None], (rows, LANES))
    seg_row = jnp.broadcast_to(named[None, :], (8, rows))

    def project(layer, stream):
        depth, cols = half, columns + LANES
        args = [core_vec, stream, *own[:3], *other[:3]]
        keep, send = call(
            functools.partial(project_kernel, layer),
            [shape(rows, cols, f32), shape(rows, cols, bf16)],
            args,
            smem=(0,),
            hbm=range(2, 8),
            scratch=[pltpu.VMEM((depth, w.shape[1]), bf16) for w in own[:3]]
            + [pltpu.SemaphoreType.DMA((3,))],
            flops=4 * rows * half * columns,
        )
        keep, *sends = add(keep, [swap(send)], 2, True)
        return sum_fsdp(keep, sends, True)

    def head_grads(layer, grad, grad_other):
        keep, *sends = call(
            functools.partial(heads_kernel, layer),
            [shape(rows, head_cols, f32)] + [shape(rows // 2, head_cols, bf16)] * 2,
            [core_vec, grad, grad_other, own[3], other[3]],
            smem=(0,),
            hbm=(3, 4),
            scratch=[pltpu.VMEM((head_cols, features), bf16), pltpu.SemaphoreType.DMA],
            flops=2 * rows * features * head_cols,
        )
        return keep, sends

    keep, (recv_a, recv_b) = project(0, stream0)
    rows0, inv0, heads0 = call(
        functools.partial(forward_kernel, group),
        [shape(rows, columns, bf16), shape(rows, LANES, f32), shape(rows, head_cols, bf16)],
        [keep, recv_a, recv_b, seg_col, seg_row],
        flops=4 * rows * BLOCK * head_cols,
    )

    top_grad, stream0 = lax.optimization_barrier((top_grad, stream0))
    grad1 = gather_tokens(top_grad)
    grad1_other = swap(grad1)
    head_keep, head_sends = head_grads(1, grad1, grad1_other)
    heads0, head_sends = lax.optimization_barrier((heads0, head_sends))

    keep, send = call(
        functools.partial(out_kernel, 0),
        [shape(rows, half, f32), shape(rows, half, bf16)],
        [core_vec, heads0, own[3], other[3]],
        smem=(0,),
        hbm=(2, 3),
        scratch=[pltpu.VMEM((head_cols, features), bf16), pltpu.SemaphoreType.DMA],
        flops=2 * rows * features * head_cols,
    )
    keep, send = call(
        halve_kernel, [shape(rows // 2, half, f32), shape(rows // 2, half, bf16)], [keep, swap(send)]
    )
    keep, send = add(keep, [exchange(send, "tp", 1)], 1, False)
    (stream1,) = call(
        stream_kernel,
        [shape(rows // 2, half, bf16)],
        [keep, exchange(send, "tp", 2), stream0[: rows // 2]],
    )
    stream1 = jnp.concatenate([stream1, exchange(stream1, "tp", 1)])
    head_keep, (head_a, head_b) = sum_fsdp(head_keep, head_sends, False)

    keep, (recv_a, recv_b) = project(1, stream1)
    inv1, heads1, grads1, dots = call(
        functools.partial(both_kernel, group),
        [
            shape(rows, LANES, f32),
            shape(rows, head_cols, bf16),
            shape(rows, columns + LANES, bf16),
            shape(rows, LANES, f32),
        ],
        [keep, recv_a, recv_b, head_keep, head_a, head_b, seg_col, seg_row],
        scratch=[
            pltpu.VMEM((rows, columns), bf16),
            pltpu.VMEM((rows, columns), f32),
            pltpu.VMEM((rows, head_cols), bf16),
        ],
        flops=14 * rows * BLOCK * head_cols,
    )
    grads1_other = swap(grads1)
    keep, send = call(
        functools.partial(normed_kernel, 1),
        [shape(rows // 2, half + LANES, f32), shape(rows // 2, half + LANES, bf16)],
        [core_vec, grads1, grads1_other, dots, *own[:3], *other[:3]],
        smem=(0,),
        hbm=range(4, 10),
        scratch=[pltpu.VMEM((half, w.shape[1]), bf16) for w in own[:3]]
        + [pltpu.VMEM((rows, half), f32), pltpu.SemaphoreType.DMA((3,))],
        flops=4 * rows * half * columns,
    )
    keep, send = add(keep, [exchange(send, "tp", 1)], 1, True)
    (grad0,) = call(
        grad_kernel,
        [shape(rows // 2, half, bf16)],
        [
            keep,
            exchange(send, "tp", 2),
            grad1[: rows // 2],
            stream1[: rows // 2],
            inv1[: rows // 2],
        ],
    )
    grad0 = jnp.concatenate([grad0, exchange(grad0, "tp", 1)])

    grad0_other = swap(grad0)
    head_keep, head_sends = head_grads(0, grad0, grad0_other)
    head_keep, (head_a, head_b) = sum_fsdp(head_keep, head_sends, False)
    (grads0,) = call(
        functools.partial(back_kernel, group),
        [shape(rows, columns, bf16)],
        [rows0, head_keep, head_a, head_b, seg_col, seg_row],
        scratch=[pltpu.VMEM((rows, head_cols), bf16)],
        flops=12 * rows * BLOCK * head_cols,
    )

    first = core == 0
    inv = jnp.where(first, inv0[:, :1], inv1[:, :1])

    def ordered(mine, theirs):
        return jnp.concatenate(
            [jnp.where(first, mine, theirs), jnp.where(first, theirs, mine)], 1
        )

    stream_other = swap(jnp.where(first, stream1, stream0))
    stream_own = jnp.where(first, stream0, stream1)
    normed = (ordered(stream_own, stream_other).astype(f32) * inv).astype(bf16)
    heads_other = swap(jnp.where(first, heads1, heads0))
    heads_all = ordered(jnp.where(first, heads0, heads1), heads_other)
    grad_all = ordered(
        jnp.where(first, grad0, grad1), jnp.where(first, grad0_other, grad1_other)
    )
    grads0_other = swap(grads0)
    grads = jnp.where(first, grads0, grads1[:, :columns])
    grads_other = jnp.where(first, grads0_other, grads1_other[:, :columns])

    def weight_grad(left, right):
        return jnp.einsum("tm,tq->mq", left, right, preferred_element_type=f32)[None]

    cuts = (slice(0, head_cols), slice(head_cols, head_cols + kv_cols), slice(head_cols + kv_cols, columns))
    query_all, key_all, value_all = (ordered(grads[:, cut], grads_other[:, cut]) for cut in cuts)
    return (
        weight_grad(normed, query_all),
        weight_grad(normed, key_all),
        weight_grad(normed, value_all),
        weight_grad(heads_all, grad_all),
    )


def solution(mesh):
    return jax.shard_map(
        local,
        mesh=mesh,
        in_specs=(
            P(None, "tp", "fsdp"),
            P(None, "tp", "fsdp"),
            P(None, "tp"),
            P(),
            P(),
            P(),
            P("pp", "fsdp", "tp"),
            P("pp", "fsdp", "tp"),
            P("pp", "fsdp", "tp"),
            P("pp", "tp", "fsdp"),
        ),
        out_specs=(
            P("pp", "fsdp", "tp"),
            P("pp", "fsdp", "tp"),
            P("pp", "fsdp", "tp"),
            P("pp", "tp", "fsdp"),
        ),
        check_vma=False,
    )
```

time: 586 us -> 268 us (0.46)
  blocking collectives: 246 us -> 0 us
  matrix products: 93.6 us -> 13.4 us
  Pallas kernels: 0 us -> 71.7 us
  other arithmetic: 56.1 us -> 18 us
  waiting for transfers between devices: 134 us -> 106 us
  starting transfers between devices: 6.07 us -> 31.2 us
  between operations: 15.5 us -> 1.23 us
    all_gather x18 -> x0, blocking collectives: 195 us -> none  [the longest x3 47.4 us: back(): grad_all = lax.all_gather(out_grad, 'tp', axis=0, tiled=True)]
    reduce_scatter x10 -> x0, waiting for transfers between devices: 133 us -> none  [the longest x2 47.5 us: finish(): lax.psum_scatter(jnp.dot(heads_all, out_layer, preferred_element_type=jnp...]
    ppermute x4 -> x41, waiting for transfers between devices: 1.1 us -> 106 us  [exchange(): lax.ppermute(value, axis, [(source, source ^ bit) for source in range(cou...]
    dot_general x50 -> x4, matrix products: 93.6 us -> 13.4 us  [weight_grad(): jnp.einsum('tm,tq->mq', left, right, preferred_element_type=f32)[None]]
    pallas_call x0 -> x20, Pallas kernels: none -> 71.7 us  [call(): pl.pallas_call(body, out_shape=list(outs), in_specs=[spec(place) for plac...]
    psum x5 -> x0, blocking collectives: 51.2 us -> none  [the longest x3 31 us: front(): squares = lax.psum(jnp.sum(stream_float * stream_float, -1), 'fsdp')]
    ppermute x4 -> x41, starting transfers between devices: 5.43 us -> 31.2 us  [exchange(): lax.ppermute(value, axis, [(source, source ^ bit) for source in range(cou...]
    scatter x19 -> x0, other arithmetic: 24.6 us -> none  [keep_item(): store.at[index_now].set(jnp.where(active, value_now, store[index_now]))]
  transfers between devices with their start and end apart: 14 -> 41, of which waited for: 11 -> 24; matrix products, arithmetic and copies ran while one was open for 17% -> 11% of each run, Pallas kernels for 0% -> 10%
where the time goes in v1:
time: 268 us; the launch traced here: 267 us
  waiting for transfers between devices  106 us (40%)
  Pallas kernels  71.7 us (27%)
  starting transfers between devices  31.2 us (12%)
  local copies, waits for them, and re-layouts  25.8 us (10%)
  other arithmetic  18 us (7%)
  matrix products  13.4 us (5%)
    ppermute x41, waiting for transfers between devices, exchange(): lax.ppermute(value, axis, [(source, source ^ bit) for source in range(cou...  106 us
    pallas_call x20, Pallas kernels, call(): pl.pallas_call(body, out_shape=list(outs), in_specs=[spec(place) for plac...  71.7 us
    ppermute x41, starting transfers between devices, exchange(): lax.ppermute(value, axis, [(source, source ^ bit) for source in range(cou...  31.2 us
    unnamed x109, local copies, waits for them, and re-layouts  14.6 us
    dot_general x4, matrix products, weight_grad(): jnp.einsum('tm,tq->mq', left, right, preferred_element_type=f32)[None]  13.4 us
    dynamic_slice x4, local copies, waits for them, and re-layouts, local(): lax.dynamic_slice_in_dim(w, (1 - core) * (w.shape[0] // 2), w.shape[0] //...  6.71 us
  transfers between devices with their start and end apart: 41, of which 24 were waited for; matrix products, arithmetic and copies ran while one was open for 11% of the time, Pallas kernels for 10%

profile of v1, /device:TPU:0, one launch (start us, length us, event | category | flops | bytes accessed | tf_op | source)
XLA Modules:
  0.0 266.8 jit_solution(3887176714741671934)
XLA Ops:
  1.6 5.1 %collective-permute-start.2 = (bf16[64,1024]{1,0:T(8,128)(2,1)S(1)}, bf16[64,1024]{1,0:T(8,128)(2,1)S(1)}, u32[]{:S(2)}, u32[]{:S(2)}) collective-permute-start(bf16[64,1024]{1,0:T(8,128)(2,1)S(1)} %bitcast.46), channel_id=1, source_target_pairs={{0,3},{1,2},{2,1},{3,0},{4,7},{5,6},{6,5},{7,4},{8,11},{9,10},{10,... | collective-permute-start | bytes 393224 | tf_op jit(solution)/shard_map/ppermute | solution.py:48
  8.6 3.3 %dynamic-slice_bitcast_fusion = bf16[512,2048]{1,0:T(8,128)(2,1)} fusion(bf16[1,1024,2048]{2,1,0:T(8,128)(2,1)} %param.20, s32[]{:T(128)S(6)} %select_n.123), kind=kLoop, calls=%fused_computation.5 | loop fusion | bytes 4194308 | tf_op jit(solution)/shard_map/dynamic_slice | solution.py:417
  24.9 8.4 %collective-permute-done = bf16[64,1024]{1,0:T(8,128)(2,1)S(1)} collective-permute-done((bf16[64,1024]{1,0:T(8,128)(2,1)S(1)}, bf16[64,1024]{1,0:T(8,128)(2,1)S(1)}, u32[]{:S(2)}, u32[]{:S(2)}) %collective-permute-start) | collective-permute-done | bytes 131104 | tf_op jit(solution)/shard_map/ppermute | solution.py:48
  35.6 5.2 %shard_map.138 = (f32[256,896]{1,0:T(8,128)}, bf16[256,896]{1,0:T(8,128)(2,1)}) custom-call(s32[1]{0:T(128)} %bitcast.2.core_ref, bf16[256,1024]{1,0:T(8,128)(2,1)} %pad_maximum_fusion.x_ref, bf16[2048,1024]{1,0:T(8,128)(2,1)} %bitcast.29, bf16[2048,256]{1,0:T(8,128)(2,1)} %bitcast.35, bf16[2048,256]{1,0:T(8,128)(2,1)} %bitcast.38, ...), custom_call_target="tpu_custom_call" | custom-call | flops 805306368 | bytes 11337732 | tf_op jit(solution)/shard_map/pallas_call | solution.py:59
  44.6 6.6 %collective-permute-done.12 = bf16[64,1024]{1,0:T(8,128)(2,1)S(1)} collective-permute-done((bf16[64,1024]{1,0:T(8,128)(2,1)S(1)}, bf16[64,1024]{1,0:T(8,128)(2,1)S(1)}, u32[]{:S(2)}, u32[]{:S(2)}) %collective-permute-start.12) | collective-permute-done | bytes 131104 | tf_op jit(solution)/shard_map/ppermute | solution.py:48
  57.7 4.3 %collective-permute-done.7.refs_0_ = bf16[128,896]{1,0:T(8,128)(2,1)S(1)} collective-permute-done((bf16[128,896]{1,0:T(8,128)(2,1)}, bf16[128,896]{1,0:T(8,128)(2,1)S(1)}, u32[]{:S(2)}, u32[]{:S(2)}) %collective-permute-start.7) | collective-permute-done | bytes 229408 | tf_op jit(solution)/shard_map/ppermute | solution.py:48
  69.7 4.4 %shard_map.142 = (f32[256,512]{1,0:T(8,128)}, bf16[128,512]{1,0:T(8,128)(2,1)}, bf16[128,512]{1,0:T(8,128)(2,1)}) custom-call(s32[1]{0:T(128)} %bitcast.2.core_ref, bf16[256,1024]{1,0:T(8,128)(2,1)} %copy-done.7, bf16[256,1024]{1,0:T(8,128)(2,1)} %copy-done.12, bf16[1024,2048]{1,0:T(8,128)(2,1)} %bitcast.32, bf16[512,2048]{1,0:T(8,128)(2,1)} %collective-permute-done.15.other), custom_call_target="tpu_custom_call" | custom-call | flops 536870912 | bytes 8126468 | tf_op jit(solution)/shard_map/pallas_call | solution.py:59
  75.6 4.9 %shard_map.141 = (bf16[256,768]{1,0:T(8,128)(2,1)}, f32[256,128]{1,0:T(8,128)}, bf16[256,512]{1,0:T(8,128)(2,1)}) custom-call(f32[256,896]{1,0:T(8,128)} %get-tuple-element.60.keep, bf16[128,896]{1,0:T(8,128)(2,1)} %copy-done.33, bf16[128,896]{1,0:T(8,128)(2,1)} %copy-done.34, s32[256,128]{1,0:T(8,128)} %broadcast_in_dim.18.seg_col, ...), custom_call_target="tpu_custom_call" | custom-call | flops 67108864 | bytes 2301952 | tf_op jit(solution)/shard_map/pallas_call | solution.py:59
  80.5 4.1 %shard_map.143 = (f32[256,1024]{1,0:T(8,128)}, bf16[256,1024]{1,0:T(8,128)(2,1)}) custom-call(s32[1]{0:T(128)} %bitcast.2.core_ref, bf16[256,512]{1,0:T(8,128)(2,1)} %get-tuple-element.67.heads, bf16[1024,2048]{1,0:T(8,128)(2,1)} %bitcast.33, bf16[512,2048]{1,0:T(8,128)(2,1)} %collective-permute-done.15.other), custom_call_target="tpu_custom_call" | custom-call | flops 536870912 | bytes 8126468 | tf_op jit(solution)/shard_map/pallas_call | solution.py:59
  90.1 8.4 %collective-permute-done.17.refs_0_ = bf16[128,1024]{1,0:T(8,128)(2,1)S(1)} collective-permute-done((bf16[128,1024]{1,0:T(8,128)(2,1)}, bf16[128,1024]{1,0:T(8,128)(2,1)S(1)}, u32[]{:S(2)}, u32[]{:S(2)}) %collective-permute-start.17) | collective-permute-done | bytes 262176 | tf_op jit(solution)/shard_map/ppermute | solution.py:48
  103.3 12.0 %collective-permute-done.18.recv = bf16[128,1024]{1,0:T(8,128)(2,1)S(1)} collective-permute-done((bf16[128,1024]{1,0:T(8,128)(2,1)}, bf16[128,1024]{1,0:T(8,128)(2,1)S(1)}, u32[]{:S(2)}, u32[]{:S(2)}) %collective-permute-start.18) | collective-permute-done | bytes 262176 | tf_op jit(solution)/shard_map/ppermute | solution.py:48
  118.0 8.4 %collective-permute-done.19 = bf16[128,1024]{1,0:T(8,128)(2,1)S(1)} collective-permute-done((bf16[128,1024]{1,0:T(8,128)(2,1)}, bf16[128,1024]{1,0:T(8,128)(2,1)S(1)}, u32[]{:S(2)}, u32[]{:S(2)}) %collective-permute-start.19) | collective-permute-done | bytes 262176 | tf_op jit(solution)/shard_map/ppermute | solution.py:48
  131.7 5.3 %shard_map.147 = (f32[256,896]{1,0:T(8,128)}, bf16[256,896]{1,0:T(8,128)(2,1)}) custom-call(s32[1]{0:T(128)} %bitcast.2.core_ref, bf16[256,1024]{1,0:T(8,128)(2,1)} %get-tuple-element.120.x_ref, bf16[2048,1024]{1,0:T(8,128)(2,1)} %bitcast.30, bf16[2048,256]{1,0:T(8,128)(2,1)} %bitcast.36, bf16[2048,256]{1,0:T(8,128)(2,1)} %bitcast.39, ...), custom_call_target="tpu_custom_call" | custom-call | flops 805306368 | bytes 11337732 | tf_op jit(solution)/shard_map/pallas_call | solution.py:59
  146.5 4.6 %collective-permute-done.22.refs_0_ = bf16[128,896]{1,0:T(8,128)(2,1)S(1)} collective-permute-done((bf16[128,896]{1,0:T(8,128)(2,1)}, bf16[128,896]{1,0:T(8,128)(2,1)S(1)}, u32[]{:S(2)}, u32[]{:S(2)}) %collective-permute-start.22) | collective-permute-done | bytes 229408 | tf_op jit(solution)/shard_map/ppermute | solution.py:48
  167.2 7.4 %shard_map.151 = (f32[256,128]{1,0:T(8,128)}, bf16[256,512]{1,0:T(8,128)(2,1)}, bf16[256,896]{1,0:T(8,128)(2,1)}, f32[256,128]{1,0:T(8,128)}) custom-call(f32[256,896]{1,0:T(8,128)} %get-tuple-element.80.keep, bf16[128,896]{1,0:T(8,128)(2,1)} %copy-done.31, bf16[128,896]{1,0:T(8,128)(2,1)} %copy-done.32, f32[256,512]{1,0:T(8,128)} %get-tuple-element.86.grad_keep, ...), custom_call_target="tpu_custom_call" | custom-call | flops 234881024 | bytes 3284992 | tf_op jit(solution)/shard_map/pallas_call | solution.py:59
  177.5 5.1 %shard_map.152 = (f32[128,1152]{1,0:T(8,128)}, bf16[128,1152]{1,0:T(8,128)(2,1)}) custom-call(s32[1]{0:T(128)} %bitcast.2.core_ref, bf16[256,896]{1,0:T(8,128)(2,1)} %get-tuple-element.91.own_grads, bf16[256,896]{1,0:T(8,128)(2,1)} %copy-done.17, f32[256,128]{1,0:T(8,128)} %get-tuple-element.92.dots, bf16[2048,1024]{1,0:T(8,128)(2,1)} %bitcast.31, ...), custom_call_target="tpu_custom_call" | custom-call | flops 805306368 | bytes 11370500 | tf_op jit(solution)/shard_map/pallas_call | solution.py:59
  182.9 9.0 %collective-permute-done.31.refs_0_ = bf16[128,1152]{1,0:T(8,128)(2,1)S(1)} collective-permute-done((bf16[128,1152]{1,0:T(8,128)(2,1)}, bf16[128,1152]{1,0:T(8,128)(2,1)S(1)}, u32[]{:S(2)}, u32[]{:S(2)}) %collective-permute-start.31) | collective-permute-done | bytes 294944 | tf_op jit(solution)/shard_map/ppermute | solution.py:48
  197.7 12.8 %collective-permute-done.32.recv = bf16[128,1152]{1,0:T(8,128)(2,1)S(1)} collective-permute-done((bf16[128,1152]{1,0:T(8,128)(2,1)}, bf16[128,1152]{1,0:T(8,128)(2,1)S(1)}, u32[]{:S(2)}, u32[]{:S(2)}) %collective-permute-start.32) | collective-permute-done | bytes 294944 | tf_op jit(solution)/shard_map/ppermute | solution.py:48
  213.5 8.4 %collective-permute-done.33 = bf16[128,1024]{1,0:T(8,128)(2,1)S(1)} collective-permute-done((bf16[128,1024]{1,0:T(8,128)(2,1)}, bf16[128,1024]{1,0:T(8,128)(2,1)S(1)}, u32[]{:S(2)}, u32[]{:S(2)}) %collective-permute-start.33) | collective-permute-done | bytes 262176 | tf_op jit(solution)/shard_map/ppermute | solution.py:48
  226.4 4.4 %shard_map.155 = (f32[256,512]{1,0:T(8,128)}, bf16[128,512]{1,0:T(8,128)(2,1)}, bf16[128,512]{1,0:T(8,128)(2,1)}) custom-call(s32[1]{0:T(128)} %bitcast.2.core_ref, bf16[256,1024]{1,0:T(8,128)(2,1)} %copy-done.11, bf16[256,1024]{1,0:T(8,128)(2,1)} %copy-done.14, bf16[1024,2048]{1,0:T(8,128)(2,1)} %bitcast.34, bf16[512,2048]{1,0:T(8,128)(2,1)} %collective-permute-done.15.other), custom_call_target="tpu_custom_call" | custom-call | flops 536870912 | bytes 8126468 | tf_op jit(solution)/shard_map/pallas_call | solution.py:59
  233.8 3.0 %collective-permute-done.35.refs_0_ = bf16[128,512]{1,0:T(8,128)(2,1)} collective-permute-done((bf16[128,512]{1,0:T(8,128)(2,1)}, bf16[128,512]{1,0:T(8,128)(2,1)}, u32[]{:S(2)}, u32[]{:S(2)}) %collective-permute-start.35) | collective-permute-done | bytes 131104 | tf_op jit(solution)/shard_map/ppermute | solution.py:48
  246.2 5.6 %shard_map.157 = bf16[256,768]{1,0:T(8,128)(2,1)} custom-call(bf16[256,768]{1,0:T(8,128)(2,1)} %get-tuple-element.90.rows, f32[256,512]{1,0:T(8,128)} %get-tuple-element.100.grad_keep, bf16[128,512]{1,0:T(8,128)(2,1)} %copy-done.43, bf16[128,512]{1,0:T(8,128)(2,1)} %copy-done.44, s32[256,128]{1,0:T(8,128)} %broadcast_in_dim.18.seg_col, ...), custom_call_target="tpu_custom_call" | custom-call | flops 201326592 | bytes 1712128 | tf_op jit(solution)/shard_map/pallas_call | solution.py:59
  253.2 4.7 %convolution_bitcast_fusion = f32[1,1024,2048]{2,1,0:T(8,128)} fusion(bf16[256,1024]{1,0:T(8,128)(2,1)S(1)} %get-tuple-element.109, bf16[256,1024]{1,0:T(8,128)(2,1)S(1)} %get-tuple-element.108, bf16[256,512]{1,0:T(8,128)(2,1)S(1)} %copy-done.20, bf16[256,512]{1,0:T(8,128)(2,1)S(1)} %get-tuple-element.112), kind=kOutput, calls=%fused_computation | convolution fusion | flops 1076887552 | bytes 9961472 | tf_op jit(solution)/shard_map/tm,tq->mq/dot_general | solution.py:578
  262.0 4.8 %convolution_bitcast_fusion.1 = f32[1,2048,1024]{2,1,0:T(8,128)} fusion(bf16[256,512]{1,0:T(8,128)(2,1)S(1)} %get-tuple-element.119, bf16[256,512]{1,0:T(8,128)(2,1)S(1)} %get-tuple-element.118, bf16[256,1024]{1,0:T(8,128)(2,1)S(1)} %get-tuple-element.111, bf16[256,1024]{1,0:T(8,128)(2,1)S(1)} %get-tuple-element.110, f32[256]{0:T(256)S(1)} %select_reduce_fusion), kind=kOutput, calls=%fused_computation.1 | convolution fusion | flops 1077936128 | bytes 9962496 | tf_op jit(solution)/shard_map/tm,tq->mq/dot_general | solution.py:578
  (246 shorter events, 115.2 us)
Async XLA Ops:
  1.6 20.9 %collective-permute-start.2 = (bf16[64,1024]{1,0:T(8,128)(2,1)S(1)}, bf16[64,1024]{1,0:T(8,128)(2,1)S(1)}, u32[]{:S(2)}, u32[]{:S(2)}) collective-permute-start(bf16[64,1024]{1,0:T(8,128)(2,1)S(1)} %bitcast.46), channel_id=1, source_target_pairs={{0,3},{1,2},{2,1},{3,0},{4,7},{5,6},{6,5},{7,4},{8,11},{9,10},{10,... | collective-permute-start | bytes 393224 | tf_op jit(solution)/shard_map/ppermute | solution.py:48
  6.7 17.4 %collective-permute-start.1 = (bf16[64,1024]{1,0:T(8,128)(2,1)S(1)}, bf16[64,1024]{1,0:T(8,128)(2,1)S(1)}, u32[]{:S(2)}, u32[]{:S(2)}) collective-permute-start(bf16[64,1024]{1,0:T(8,128)(2,1)S(1)} %bitcast.47), channel_id=1, source_target_pairs={{0,1},{1,0},{2,3},{3,2},{4,5},{5,4},{6,7},{7,6},{8,9},{9,8},{10,11... | collective-permute-start | bytes 393224 | tf_op jit(solution)/shard_map/ppermute | solution.py:48
  8.6 25.5 %collective-permute-start.5 = (bf16[1024,256]{1,0:T(8,128)(2,1)}, bf16[1024,256]{1,0:T(8,128)(2,1)}, u32[]{:S(2)}, u32[]{:S(2)}) collective-permute-start(bf16[1024,256]{1,0:T(8,128)(2,1)} %dynamic-slice_bitcast_fusion.2), channel_id=1, source_target_pairs={{0,16},{16,0},{1,17},{17,1},{2,18},{18,2},{3,19},{19,3},{4,20},{20... | collective-permute-start | bytes 1572872 | tf_op jit(solution)/shard_map/ppermute | solution.py:48
  11.9 57.0 %collective-permute-start.15 = (bf16[512,2048]{1,0:T(8,128)(2,1)}, bf16[512,2048]{1,0:T(8,128)(2,1)}, u32[]{:S(2)}, u32[]{:S(2)}) collective-permute-start(bf16[512,2048]{1,0:T(8,128)(2,1)} %dynamic-slice_bitcast_fusion), channel_id=1, source_target_pairs={{0,16},{16,0},{1,17},{17,1},{2,18},{18,2},{3,19},{19,3},{4,20},{20... | collective-permute-start | bytes 6291464 | tf_op jit(solution)/shard_map/ppermute | solution.py:48
  14.0 20.2 %collective-permute-start.3 = (bf16[1024,1024]{1,0:T(8,128)(2,1)}, bf16[1024,1024]{1,0:T(8,128)(2,1)S(1)}, u32[]{:S(2)}, u32[]{:S(2)}) collective-permute-start(bf16[1024,1024]{1,0:T(8,128)(2,1)} %dynamic-slice_bitcast_fusion.1), channel_id=1, source_target_pairs={{0,16},{16,0},{1,17},{17,1},{2,18},{18,2},{3,19},{19,3},{4,20},{20... | collective-permute-start | bytes 6291464 | tf_op jit(solution)/shard_map/ppermute | solution.py:48
  22.5 11.6 %collective-permute-start.4 = (bf16[1024,256]{1,0:T(8,128)(2,1)S(1)}, bf16[1024,256]{1,0:T(8,128)(2,1)S(1)}, u32[]{:S(2)}, u32[]{:S(2)}) collective-permute-start(bf16[1024,256]{1,0:T(8,128)(2,1)S(1)} %dynamic-slice_bitcast_fusion.3), channel_id=1, source_target_pairs={{0,16},{16,0},{1,17},{17,1},{2,18},{18,2},{3,19},{19,3},{4,20},{20... | collective-permute-start | bytes 1572872 | tf_op jit(solution)/shard_map/ppermute | solution.py:48
  24.1 9.2 %collective-permute-start = (bf16[64,1024]{1,0:T(8,128)(2,1)S(1)}, bf16[64,1024]{1,0:T(8,128)(2,1)S(1)}, u32[]{:S(2)}, u32[]{:S(2)}) collective-permute-start(bf16[64,1024]{1,0:T(8,128)(2,1)S(1)} %bitcast.48), channel_id=1, source_target_pairs={{0,2},{1,3},{2,0},{3,1},{4,6},{5,7},{6,4},{7,5},{8,10},{9,11},{10,... | collective-permute-start | bytes 393224 | tf_op jit(solution)/shard_map/ppermute | solution.py:48
  34.1 10.4 %collective-permute-start.11 = (bf16[64,1024]{1,0:T(8,128)(2,1)S(1)}, bf16[64,1024]{1,0:T(8,128)(2,1)S(1)}, u32[]{:S(2)}, u32[]{:S(2)}) collective-permute-start(bf16[64,1024]{1,0:T(8,128)(2,1)S(1)} %bitcast.41), channel_id=1, source_target_pairs={{0,2},{1,3},{2,0},{3,1},{4,6},{5,7},{6,4},{7,5},{8,10},{9,11},{10,... | collective-permute-start | bytes 393224 | tf_op jit(solution)/shard_map/ppermute | solution.py:48
  40.9 10.3 %collective-permute-start.6 = (bf16[256,896]{1,0:T(8,128)(2,1)}, bf16[256,896]{1,0:T(8,128)(2,1)S(1)}, u32[]{:S(2)}, u32[]{:S(2)}) collective-permute-start(bf16[256,896]{1,0:T(8,128)(2,1)} %get-tuple-element.56), channel_id=1, source_target_pairs={{0,16},{16,0},{1,17},{17,1},{2,18},{18,2},{3,19},{19,3},{4,20},{20... | collective-permute-start | bytes 1376264 | tf_op jit(solution)/shard_map/ppermute | solution.py:48
  41.1 16.6 %collective-permute-start.13 = (bf16[64,1024]{1,0:T(8,128)(2,1)S(1)}, bf16[64,1024]{1,0:T(8,128)(2,1)S(1)}, u32[]{:S(2)}, u32[]{:S(2)}) collective-permute-start(bf16[64,1024]{1,0:T(8,128)(2,1)S(1)} %bitcast.42), channel_id=1, source_target_pairs={{0,3},{1,2},{2,1},{3,0},{4,7},{5,6},{6,5},{7,4},{8,11},{9,10},{10,... | collective-permute-start | bytes 393224 | tf_op jit(solution)/shard_map/ppermute | solution.py:48
  42.7 8.5 %collective-permute-start.12 = (bf16[64,1024]{1,0:T(8,128)(2,1)S(1)}, bf16[64,1024]{1,0:T(8,128)(2,1)S(1)}, u32[]{:S(2)}, u32[]{:S(2)}) collective-permute-start(bf16[64,1024]{1,0:T(8,128)(2,1)S(1)} %bitcast.43), channel_id=1, source_target_pairs={{0,1},{1,0},{2,3},{3,2},{4,5},{5,4},{6,7},{7,6},{8,9},{9,8},{10,11... | collective-permute-start | bytes 393224 | tf_op jit(solution)/shard_map/ppermute | solution.py:48
  57.6 11.3 %collective-permute-start.14 = (bf16[256,1024]{1,0:T(8,128)(2,1)S(1)}, bf16[256,1024]{1,0:T(8,128)(2,1)S(1)}, u32[]{:S(2)}, u32[]{:S(2)}) collective-permute-start(bf16[256,1024]{1,0:T(8,128)(2,1)S(1)} %constant_dynamic-update-slice_fusion.own_grad), channel_id=1, source_target_pairs={{0,16},{16,0},{1,17},{17,1},{2,18},{18,2},{3,19},{19,3},{4,20},{20... | collective-permute-start | bytes 1572872 | tf_op jit(solution)/shard_map/ppermute | solution.py:48
  89.9 8.6 %collective-permute-start.17 = (bf16[128,1024]{1,0:T(8,128)(2,1)}, bf16[128,1024]{1,0:T(8,128)(2,1)S(1)}, u32[]{:S(2)}, u32[]{:S(2)}) collective-permute-start(bf16[128,1024]{1,0:T(8,128)(2,1)} %get-tuple-element.71), channel_id=1, source_target_pairs={{0,1},{1,0},{2,3},{3,2},{4,5},{5,4},{6,7},{7,6},{8,9},{9,8},{10,11... | collective-permute-start | bytes 786440 | tf_op jit(solution)/shard_map/ppermute | solution.py:48
  101.3 14.1 %collective-permute-start.18 = (bf16[128,1024]{1,0:T(8,128)(2,1)}, bf16[128,1024]{1,0:T(8,128)(2,1)S(1)}, u32[]{:S(2)}, u32[]{:S(2)}) collective-permute-start(bf16[128,1024]{1,0:T(8,128)(2,1)} %get-tuple-element.73), channel_id=1, source_target_pairs={{0,2},{1,3},{2,0},{3,1},{4,6},{5,7},{6,4},{7,5},{8,10},{9,11},{10,... | collective-permute-start | bytes 786440 | tf_op jit(solution)/shard_map/ppermute | solution.py:48
  142.4 8.7 %collective-permute-start.22 = (bf16[128,896]{1,0:T(8,128)(2,1)}, bf16[128,896]{1,0:T(8,128)(2,1)S(1)}, u32[]{:S(2)}, u32[]{:S(2)}) collective-permute-start(bf16[128,896]{1,0:T(8,128)(2,1)} %get-tuple-element.78), channel_id=1, source_target_pairs={{0,4},{4,0},{8,12},{12,8},{1,5},{5,1},{9,13},{13,9},{2,6},{6,2},{1... | collective-permute-start | bytes 688136 | tf_op jit(solution)/shard_map/ppermute | solution.py:48
  143.9 8.7 %collective-permute-start.23 = (bf16[128,896]{1,0:T(8,128)(2,1)}, bf16[128,896]{1,0:T(8,128)(2,1)S(1)}, u32[]{:S(2)}, u32[]{:S(2)}) collective-permute-start(bf16[128,896]{1,0:T(8,128)(2,1)} %get-tuple-element.79), channel_id=1, source_target_pairs={{0,8},{4,12},{8,0},{12,4},{1,9},{5,13},{9,1},{13,5},{2,10},{6,14},... | collective-permute-start | bytes 688136 | tf_op jit(solution)/shard_map/ppermute | solution.py:48
  144.4 12.6 %collective-permute-start.26 = (bf16[128,512]{1,0:T(8,128)(2,1)S(1)}, bf16[128,512]{1,0:T(8,128)(2,1)S(1)}, u32[]{:S(2)}, u32[]{:S(2)}) collective-permute-start(bf16[128,512]{1,0:T(8,128)(2,1)S(1)} %copy-done.50), channel_id=1, source_target_pairs={{0,4},{4,0},{8,12},{12,8},{1,5},{5,1},{9,13},{13,9},{2,6},{6,2},{1... | collective-permute-start | bytes 393224 | tf_op jit(solution)/shard_map/ppermute | solution.py:48
  145.0 12.0 %collective-permute-start.27 = (bf16[128,512]{1,0:T(8,128)(2,1)S(1)}, bf16[128,512]{1,0:T(8,128)(2,1)S(1)}, u32[]{:S(2)}, u32[]{:S(2)}) collective-permute-start(bf16[128,512]{1,0:T(8,128)(2,1)S(1)} %copy-done.49), channel_id=1, source_target_pairs={{0,8},{4,12},{8,0},{12,4},{1,9},{5,13},{9,1},{13,5},{2,10},{6,14},... | collective-permute-start | bytes 393224 | tf_op jit(solution)/shard_map/ppermute | solution.py:48
  155.8 10.5 %collective-permute-start.24 = (bf16[128,896]{1,0:T(8,128)(2,1)}, bf16[128,896]{1,0:T(8,128)(2,1)S(1)}, u32[]{:S(2)}, u32[]{:S(2)}) collective-permute-start(bf16[128,896]{1,0:T(8,128)(2,1)} %get-tuple-element.81), channel_id=1, source_target_pairs={{0,8},{4,12},{8,0},{12,4},{1,9},{5,13},{9,1},{13,5},{2,10},{6,14},... | collective-permute-start | bytes 688136 | tf_op jit(solution)/shard_map/ppermute | solution.py:48
  156.3 10.0 %collective-permute-start.25 = (bf16[128,896]{1,0:T(8,128)(2,1)}, bf16[128,896]{1,0:T(8,128)(2,1)S(1)}, u32[]{:S(2)}, u32[]{:S(2)}) collective-permute-start(bf16[128,896]{1,0:T(8,128)(2,1)} %get-tuple-element.82), channel_id=1, source_target_pairs={{0,4},{4,0},{8,12},{12,8},{1,5},{5,1},{9,13},{13,9},{2,6},{6,2},{1... | collective-permute-start | bytes 688136 | tf_op jit(solution)/shard_map/ppermute | solution.py:48
  182.6 9.3 %collective-permute-start.31 = (bf16[128,1152]{1,0:T(8,128)(2,1)}, bf16[128,1152]{1,0:T(8,128)(2,1)S(1)}, u32[]{:S(2)}, u32[]{:S(2)}) collective-permute-start(bf16[128,1152]{1,0:T(8,128)(2,1)} %get-tuple-element.94), channel_id=1, source_target_pairs={{0,1},{1,0},{2,3},{3,2},{4,5},{5,4},{6,7},{7,6},{8,9},{9,8},{10,11... | collective-permute-start | bytes 884744 | tf_op jit(solution)/shard_map/ppermute | solution.py:48
  194.9 15.6 %collective-permute-start.32 = (bf16[128,1152]{1,0:T(8,128)(2,1)}, bf16[128,1152]{1,0:T(8,128)(2,1)S(1)}, u32[]{:S(2)}, u32[]{:S(2)}) collective-permute-start(bf16[128,1152]{1,0:T(8,128)(2,1)} %get-tuple-element.96), channel_id=1, source_target_pairs={{0,2},{1,3},{2,0},{3,1},{4,6},{5,7},{6,4},{7,5},{8,10},{9,11},{10,... | collective-permute-start | bytes 884744 | tf_op jit(solution)/shard_map/ppermute | solution.py:48
  213.5 8.4 %collective-permute-start.33 = (bf16[128,1024]{1,0:T(8,128)(2,1)}, bf16[128,1024]{1,0:T(8,128)(2,1)S(1)}, u32[]{:S(2)}, u32[]{:S(2)}) collective-permute-start(bf16[128,1024]{1,0:T(8,128)(2,1)} %shard_map.154), channel_id=1, source_target_pairs={{0,1},{1,0},{2,3},{3,2},{4,5},{5,4},{6,7},{7,6},{8,9},{9,8},{10,11... | collective-permute-start | bytes 786440 | tf_op jit(solution)/shard_map/ppermute | solution.py:48
  223.7 17.3 %collective-permute-start.40 = (bf16[256,512]{1,0:T(8,128)(2,1)S(1)}, bf16[256,512]{1,0:T(8,128)(2,1)}, u32[]{:S(2)}, u32[]{:S(2)}) collective-permute-start(bf16[256,512]{1,0:T(8,128)(2,1)S(1)} %broadcast_select_fusion.10), channel_id=1, source_target_pairs={{0,16},{16,0},{1,17},{17,1},{2,18},{18,2},{3,19},{19,3},{4,20},{20... | collective-permute-start | bytes 786440 | tf_op jit(solution)/shard_map/ppermute | solution.py:48
  (69 other events, 402.6 us)
